TPU v7x, 1024 devices: a whole 8x8x8 slice. The times are simulated.
1024 devices in a mesh: dp: 128 (over y, z_lo, x), seq: 8 (over z_hi, core).
Axes of the slice: x: 8, y: 8, z: 8 (z_hi: 4, z_lo: 2; z = z_hi * 2 + z_lo), core: 2. Of those that a mesh axis runs over, the one named last changes fastest.
Arguments:
- cotangent: bfloat16 [128, 1024, 2048], P('dp', 'seq'), may hold values from -0.875 to 0.875
- expert_ids: int32 [128, 1024, 2], P('dp', 'seq'), may hold values from 0 to 15, as said below
- gate_probs: float32 [128, 1024, 2], P('dp', 'seq'), may hold values from 0.05 to 1
- hidden_acts: bfloat16 [7168, 16384], P('seq', 'dp'), may hold values from -6 to 6
- step_input: bfloat16 [128, 1024, 256], P('dp', 'seq'), may hold values from -6 to 6
- step_proj: bfloat16 [256, 4096], replicated, may hold values from -0.375 to 0.375
- step_bias: float32 [4096], replicated, may hold values from -1 to 1
- decay_rate: float32 [16, 4096], replicated, may hold values from 0.00048828125 to 0.05
- input_coef: float32 [128, 16, 1024], P('dp', None, 'seq'), may hold values from -4 to 4
- output_coef: float32 [128, 16, 1024], P('dp', None, 'seq'), may hold values from -0.5 to 0.5
- grad_output: bfloat16 [128, 1024, 4096], P('dp', 'seq'), may hold values from -6 to 6
- skip_weight: float32 [4096], replicated, may hold values from 0.5 to 1.5
Outputs:
- grad_down: float32 [2048, 7168], P('dp', 'seq')
- grad_x: bfloat16 [128, 1024, 4096], P('dp', 'seq')
Inputs may be any that keep to these rules, and one draw needn't show every extreme that they name: `expert_ids`: each token names 2 different experts; among the tokens of one device (aligned blocks of 128 tokens of a sequence) every expert is named by exactly 16 of the pairs.
All inputs are finite; a program needn't handle non-finite values.
Results may differ from a plain program's by a relative error of at most 0.0029.
Values may be sent and summed in bfloat16 or wider, within the bound.
A program may use at most 64 MiB of HBM per device.

v0:
```python
import jax
import jax.numpy as jnp
from jax import lax
from jax.sharding import PartitionSpec as P

BLOCK = 16


def from_behind(value, axis, by):
    peers = lax.axis_size(axis)
    pairs = [(i, i + by) for i in range(peers) if 0 <= i + by < peers]
    return lax.ppermute(value, axis, pairs)


def on_device(
    cotangent,
    expert_ids,
    gate_probs,
    hidden_acts,
    step_input,
    step_proj,
    step_bias,
    decay_rate,
    input_coef,
    output_coef,
    grad_output,
    skip_weight,
):
    tok_count = cotangent.shape[1]
    top_count = expert_ids.shape[2]
    pair_count = tok_count * top_count
    capacity = hidden_acts.shape[1] // lax.axis_size("seq")
    chosen = (expert_ids.reshape(pair_count) == 0).astype(jnp.int32)
    before = jnp.cumsum(chosen) - chosen
    destination = jnp.where(chosen == 1, before, capacity)
    token_of_slot = (
        jnp.zeros((capacity + 1,), jnp.int32)
        .at[destination]
        .set(jnp.arange(pair_count, dtype=jnp.int32) // top_count)[:capacity]
    )
    gate_of_slot = (
        jnp.zeros((capacity + 1,), jnp.float32)
        .at[destination]
        .set(gate_probs.reshape(pair_count))[:capacity]
    )
    picked = cotangent[0][token_of_slot]
    routed_local = (picked.astype(jnp.float32) * gate_of_slot[:, None]).astype(jnp.bfloat16)
    channels = grad_output.shape[2]
    state_size = decay_rate.shape[0]
    step_size = jax.nn.softplus(
        jnp.dot(step_input[0], step_proj, preferred_element_type=jnp.float32) + step_bias[None, :]
    )
    negative_rate = -decay_rate
    block_count = tok_count // BLOCK
    step_blocks = step_size.reshape(block_count, BLOCK, channels)
    grad_blocks = grad_output[0].reshape(block_count, BLOCK, channels)
    in_blocks = jnp.transpose(input_coef[0].reshape(state_size, block_count, BLOCK), (1, 0, 2))
    out_blocks = jnp.transpose(output_coef[0].reshape(state_size, block_count, BLOCK), (1, 0, 2))

    def block_step(state_carry, inputs):
        step_rows, grad_rows, in_cols, out_cols = inputs
        results = [None] * BLOCK
        for position in reversed(range(BLOCK)):
            out_grad = grad_rows[position].astype(jnp.float32)
            adjoint = out_cols[:, position][:, None] * out_grad[None, :] + state_carry
            results[position] = (
                step_rows[position] * jnp.sum(in_cols[:, position][:, None] * adjoint, axis=0)
                + skip_weight * out_grad
            )
            state_carry = jnp.exp(step_rows[position][None, :] * negative_rate) * adjoint
        return (state_carry, jnp.stack(results))

    outgoing, local_rows = lax.scan(
        block_step,
        jnp.zeros((state_size, channels), jnp.float32),
        (step_blocks, grad_blocks, in_blocks, out_blocks),
        reverse=True,
    )
    local_rows = local_rows.reshape(tok_count, channels)
    step_total = jnp.sum(step_size, axis=0)
    passing = jnp.exp(negative_rate * step_total[None, :])

    def relay_step(counter, pair_state):
        sending, received = pair_state
        received = from_behind(sending, "seq", -1)
        return (outgoing + passing * received, received)

    unused, incoming = lax.fori_loop(
        0, lax.axis_size("seq") - 1, relay_step, (outgoing, jnp.zeros_like(outgoing))
    )
    row_ids = lax.broadcasted_iota(jnp.int32, (tok_count, tok_count), 0)
    col_ids = lax.broadcasted_iota(jnp.int32, (tok_count, tok_count), 1)
    strict_upper = (col_ids > row_ids).astype(jnp.float32)
    later_sum = jnp.dot(
        strict_upper, step_size, precision=lax.Precision.HIGHEST, preferred_element_type=jnp.float32
    )
    carried = jnp.zeros((tok_count, channels), jnp.float32)
    for state_row in range(state_size):
        carried = (
            carried
            + input_coef[0][state_row][:, None]
            * jnp.exp(negative_rate[state_row][None, :] * later_sum)
            * incoming[state_row][None, :]
        )
    grad_x = (local_rows + step_size * carried).astype(jnp.bfloat16)[None]
    dense_term = lax.dot_general(
        lax.all_gather(routed_local, "seq", axis=0, tiled=True),
        hidden_acts,
        (((0,), (1,)), ((), ())),
        preferred_element_type=jnp.float32,
    )
    grad_down = lax.psum_scatter(dense_term, "dp", scatter_dimension=0, tiled=True)
    return (grad_down, grad_x)


def solution(mesh):
    return jax.shard_map(
        on_device,
        mesh=mesh,
        in_specs=(
            P("dp", "seq", None),
            P("dp", "seq", None),
            P("dp", "seq", None),
            P("seq", "dp"),
            P("dp", "seq", None),
            P(),
            P(),
            P(),
            P("dp", None, "seq"),
            P("dp", None, "seq"),
            P("dp", "seq", None),
            P(),
        ),
        out_specs=(P("dp", "seq"), P("dp", "seq", None)),
        check_vma=False,
    )
```

profile of v0, /device:TPU:256, one launch (start us, length us, event | category | flops | bytes accessed | tf_op | source)
XLA Modules:
  0.0 688.9 jit_solution(10909433027774873956)
XLA Ops:
  14.7 23.1 %all_gather.3 = bf16[128,2048]{1,0:T(8,128)(2,1)S(1)} all-gather(bf16[16,2048]{1,0:T(8,128)(2,1)S(1)} %multiply_convert_fusion), channel_id=1, replica_groups=mesh['dp'=128,'seq'=8] {'seq'}, dimensions={0}, use_global_device_ids=true | all-gather | bytes 589824 | tf_op jit(solution)/shard_map/all_gather | solution.py:107
  37.8 5.1 fusion.29
  45.0 2.9 fusion.28
  49.5 99.7 %while.30 = (s32[]{:T(128)}, f32[16,4096]{1,0:T(8,128)S(1)}, f32[8,16,4096]{2,1,0:T(8,128)}, f32[8,16,4096]{2,1,0:T(8,128)}, f32[16,4096]{1,0:T(8,128)S(1)}, /*i...) while((s32[]{:T(128)}, f32[16,4096]{1,0:T(8,128)S(1)}, ...), condition=%wide.region_22.23_spmd.clone, body=%wide.region_5.22_spmd.clone.sunk | while | flops 9633811 | bytes 8400216 | solution.py:73
  50.2 2.1 dynamic-slice_convert_fusion.17
  52.4 2.3 constant_dynamic-slice_fusion.23
  63.1 2.1 dynamic-slice_convert_fusion.17
  65.2 2.1 constant_dynamic-slice_fusion.23
  87.9 2.2 dynamic-slice_convert_fusion.17
  102.2 2.1 constant_dynamic-slice_fusion.23
  114.6 2.0 constant_dynamic-slice_fusion.23
  124.9 2.2 dynamic-slice_convert_fusion.17
  137.4 2.2 dynamic-slice_convert_fusion.17
  139.6 1.9 constant_dynamic-slice_fusion.23
  149.5 72.5 %while.29 = (s32[]{:T(128)}, f32[16,4096]{1,0:T(8,128)S(1)}, f32[16,4096]{1,0:T(8,128)}, f32[16,4096]{1,0:T(8,128)S(1)}, f32[16,4096]{1,0:T(8,128)S(1)}, /*index=5*/s32[]{:T(128)}) while((s32[]{:T(128)}, f32[16,4096]{1,0:T(8,128)S(1)}, f32[16,4096]{1,0:T(8,128)}, f32[16,4096]{1,0:T(8,128)S(1)}, f32[16,4096]{1,0:T(8,128)S(1)}, ...), condition=%wide.region_25.26_spmd, body=%wide.region_24.25_spmd.sunk | while | flops 131074 | bytes 3145865 | solution.py:88
  149.5 3.4 collective-permute-start
  152.9 5.7 collective-permute-done
  159.3 4.8 collective-permute-start
  164.1 4.4 collective-permute-done
  169.1 4.7 collective-permute-start
  173.8 4.0 collective-permute-done
  178.5 4.8 collective-permute-start
  183.4 5.1 collective-permute-done
  189.2 5.1 collective-permute-start
  194.3 4.7 collective-permute-done
  199.7 5.1 collective-permute-start
  204.8 4.9 collective-permute-done
  210.4 5.1 collective-permute-start
  215.5 5.8 collective-permute-done
  222.0 2.4 fusion.27
  224.4 12.3 %fusion.21 = bf16[1,128,4096]{2,1,0:T(8,128)(2,1)} fusion(f32[128,4096]{1,0:T(8,128)} %bitcast.544, f32[4096]{0:T(1024)S(1)} %bitcast.563, f32[4096]{0:T(1024)S(1)} %bitcast.561, f32[128]{0:T(128)S(1)} %get-tuple-element.423, f32[4096]{0:T(1024)S(1)} %bitcast.564, f32[4096]{0:T(1024)S(1)} %bitcast.547, f32[128]{0:T(128)S(1)} %get-tuple-element.424, ...), kind=kOutput, calls=%fused_computation.163 | convolution fusion | flops 839925760 | bytes 5775360 | tf_op jit(solution)/shard_map/dot_general | solution.py:94
  236.7 445.4 %reduce-scatter.2.cloned.1.call-done = f32[16,896]{1,0:T(8,128)} async-done(((f32[2048,896]{1,0:T(8,128)}), f32[16,896]{1,0:T(8,128)}) %reduce-scatter.2.cloned.1.call-update) | async-done | bytes 57360 | tf_op jit(solution)/shard_map/reduce_scatter | solution.py:112
  (191 shorter events, 94.1 us)
Async XLA Ops:
  7.2 37.8 %copy-start = (bf16[256,4096]{1,0:T(8,128)(2,1)S(1)}, bf16[256,4096]{1,0:T(8,128)(2,1)}, u32[]{:S(2)}) copy-start(bf16[256,4096]{1,0:T(8,128)(2,1)} %param.21) | copy-start | bytes 6291460
  7.2 674.9 %reduce-scatter.2.cloned.1.call-start = ((), (), s32[]{:S(2)}) async-start(), calls=%async_computation.1 | async-start | bytes 7397376 | tf_op jit(solution)/shard_map/reduce_scatter | solution.py:112
  42.8 0.7 copy-start.5
  42.9 1.4 copy-start.4
  42.9 2.1 copy-start.6
  42.9 2.1 copy-start.7
  45.0 2.9 copy-start.3
  47.9 1.6 copy-start.1
  149.5 9.1 %collective-permute-start = (f32[16,4096]{1,0:T(8,128)S(1)}, f32[16,4096]{1,0:T(8,128)S(1)}, u32[]{:S(2)}, u32[]{:S(2)}) collective-permute-start(f32[16,4096]{1,0:T(8,128)S(1)} %get-tuple-element.803), channel_id=1, source_target_pairs={{1,0},{2,1},{3,2},{4,3},{5,4},{6,5},{7,6},{9,8},{10,9},{11,10},{12... | collective-permute-start | bytes 786440 | tf_op jit(solution)/shard_map/while/body/eval_jaxpr/ppermute | solution.py:12
  158.6 0.7 copy-start.2
  159.3 9.1 %collective-permute-start = (f32[16,4096]{1,0:T(8,128)S(1)}, f32[16,4096]{1,0:T(8,128)S(1)}, u32[]{:S(2)}, u32[]{:S(2)}) collective-permute-start(f32[16,4096]{1,0:T(8,128)S(1)} %get-tuple-element.803), channel_id=1, source_target_pairs={{1,0},{2,1},{3,2},{4,3},{5,4},{6,5},{7,6},{9,8},{10,9},{11,10},{12... | collective-permute-start | bytes 786440 | tf_op jit(solution)/shard_map/while/body/eval_jaxpr/ppermute | solution.py:12
  168.4 0.7 copy-start.2
  169.1 8.7 %collective-permute-start = (f32[16,4096]{1,0:T(8,128)S(1)}, f32[16,4096]{1,0:T(8,128)S(1)}, u32[]{:S(2)}, u32[]{:S(2)}) collective-permute-start(f32[16,4096]{1,0:T(8,128)S(1)} %get-tuple-element.803), channel_id=1, source_target_pairs={{1,0},{2,1},{3,2},{4,3},{5,4},{6,5},{7,6},{9,8},{10,9},{11,10},{12... | collective-permute-start | bytes 786440 | tf_op jit(solution)/shard_map/while/body/eval_jaxpr/ppermute | solution.py:12
  177.8 0.7 copy-start.2
  178.5 9.9 %collective-permute-start = (f32[16,4096]{1,0:T(8,128)S(1)}, f32[16,4096]{1,0:T(8,128)S(1)}, u32[]{:S(2)}, u32[]{:S(2)}) collective-permute-start(f32[16,4096]{1,0:T(8,128)S(1)} %get-tuple-element.803), channel_id=1, source_target_pairs={{1,0},{2,1},{3,2},{4,3},{5,4},{6,5},{7,6},{9,8},{10,9},{11,10},{12... | collective-permute-start | bytes 786440 | tf_op jit(solution)/shard_map/while/body/eval_jaxpr/ppermute | solution.py:12
  188.5 0.7 copy-start.2
  189.2 9.8 %collective-permute-start = (f32[16,4096]{1,0:T(8,128)S(1)}, f32[16,4096]{1,0:T(8,128)S(1)}, u32[]{:S(2)}, u32[]{:S(2)}) collective-permute-start(f32[16,4096]{1,0:T(8,128)S(1)} %get-tuple-element.803), channel_id=1, source_target_pairs={{1,0},{2,1},{3,2},{4,3},{5,4},{6,5},{7,6},{9,8},{10,9},{11,10},{12... | collective-permute-start | bytes 786440 | tf_op jit(solution)/shard_map/while/body/eval_jaxpr/ppermute | solution.py:12
  199.0 0.7 copy-start.2
  199.7 10.0 %collective-permute-start = (f32[16,4096]{1,0:T(8,128)S(1)}, f32[16,4096]{1,0:T(8,128)S(1)}, u32[]{:S(2)}, u32[]{:S(2)}) collective-permute-start(f32[16,4096]{1,0:T(8,128)S(1)} %get-tuple-element.803), channel_id=1, source_target_pairs={{1,0},{2,1},{3,2},{4,3},{5,4},{6,5},{7,6},{9,8},{10,9},{11,10},{12... | collective-permute-start | bytes 786440 | tf_op jit(solution)/shard_map/while/body/eval_jaxpr/ppermute | solution.py:12
  209.7 0.7 copy-start.2
  210.4 10.9 %collective-permute-start = (f32[16,4096]{1,0:T(8,128)S(1)}, f32[16,4096]{1,0:T(8,128)S(1)}, u32[]{:S(2)}, u32[]{:S(2)}) collective-permute-start(f32[16,4096]{1,0:T(8,128)S(1)} %get-tuple-element.803), channel_id=1, source_target_pairs={{1,0},{2,1},{3,2},{4,3},{5,4},{6,5},{7,6},{9,8},{10,9},{11,10},{12... | collective-permute-start | bytes 786440 | tf_op jit(solution)/shard_map/while/body/eval_jaxpr/ppermute | solution.py:12
  221.3 0.7 copy-start.2
Sparse Core Ops, SparseCore 0:
  43.0 639.0 reduce-scatter.1
where the time goes:
time: 691 us; the launch traced here: 689 us
  waiting for transfers between devices  480 us (69%)
  other arithmetic  69.6 us (10%)
  local copies, waits for them, and re-layouts  48 us (7%)
  starting transfers between devices  33 us (5%)
  blocking collectives  23.1 us (3%)
  matrix products  20.2 us (3%)
  between operations  14.1 us (2%)
    reduce_scatter x1, waiting for transfers between devices, on_device(): lax.psum_scatter(dense_term, 'dp', scatter_dimension=0, tiled=True)  445 us
    ppermute x7, waiting for transfers between devices, from_behind(): return lax.ppermute(value, axis, pairs)  34.5 us
    ppermute x7, starting transfers between devices, from_behind(): return lax.ppermute(value, axis, pairs)  33 us
    add x40, other arithmetic, block_step(): step_rows[position]  32.8 us
    all_gather x1, blocking collectives, on_device(): lax.all_gather(routed_local, 'seq', axis=0, tiled=True)  23.1 us
    reduce_sum x32, other arithmetic, block_step(): jnp.sum(in_cols[:, position][:, None] * adjoint, axis=0)  17.9 us
    convert_element_type x8, other arithmetic, block_step(): out_grad = grad_rows[position].astype(jnp.float32)  16.4 us
    slice x8, local copies, waits for them, and re-layouts, block_step(): step_rows[position][None, :] * negative_rate  16.1 us
  transfers between devices with their start and end apart: 8, of which 8 were waited for; matrix products, arithmetic and copies ran while one was open for 17% of the time, Pallas kernels for 0%

commit v1 on v0

v1 whole, which is shorter than its diff:
```python
import functools
import math

import jax
import jax.numpy as jnp
from jax import lax
from jax.experimental import pallas as pl
from jax.experimental.pallas import tpu as pltpu
from jax.sharding import PartitionSpec as P

MESH = pl.DeviceIdType.MESH
LANES = 128
TILE = 8 * LANES
LOG2E = math.log2(math.e)
UNROLL = 8
X_SIZE = 8
Y_SIZE = 8
PEERS = 8
SLOTS = 16
VMEM_LIMIT = 40 << 20


def softplus(v):
    return jnp.maximum(v, 0.0) + jnp.log1p(jnp.exp(-jnp.abs(v)))


def route(ids_ref, gate_ref, cot_ref, routed_ref):
    tokens = cot_ref.shape[0]
    named = (ids_ref[...] == 0).astype(jnp.float32)
    chosen = jnp.sum(named, axis=1, keepdims=True)
    gate = jnp.sum(named * gate_ref[...], axis=1, keepdims=True)
    row = lax.broadcasted_iota(jnp.int32, (tokens, tokens), 0)
    col = lax.broadcasted_iota(jnp.int32, (tokens, tokens), 1)
    earlier = jnp.where(col < row, 1.0, 0.0).astype(jnp.bfloat16)
    spread = jnp.broadcast_to(chosen, (tokens, LANES))
    rank = jnp.dot(earlier, spread.astype(jnp.bfloat16), preferred_element_type=jnp.float32)
    lane = lax.broadcasted_iota(jnp.int32, (tokens, LANES), 1).astype(jnp.float32)
    pick = jnp.where(rank == lane, spread, 0.0)[:, :SLOTS].astype(jnp.bfloat16)
    scaled = (cot_ref[...].astype(jnp.float32) * gate).astype(jnp.bfloat16)
    routed = lax.dot_general(
        pick, scaled, (((0,), (0,)), ((), ())), preferred_element_type=jnp.float32
    ).astype(jnp.bfloat16)
    width = routed_ref.shape[2]
    for y in range(routed_ref.shape[0]):
        routed_ref[y] = routed[:, y * width : (y + 1) * width]


def first_kernel(
    out_coef, ids_ref, gate_ref, cot_ref, x_ref, w_ref, b_ref, d_ref, g_ref,
    routed_ref, step_ref, message_ref, rate_ref, grads, state,
):
    tokens, states, tiles = x_ref.shape[0], d_ref.shape[0], TILE // LANES

    @pl.when(pl.program_id(0) == 0)
    def _():
        route(ids_ref, gate_ref, cot_ref, routed_ref)

    step = softplus(
        jnp.dot(x_ref[...], w_ref[...], preferred_element_type=jnp.float32) + b_ref[...]
    )
    g = g_ref[...].astype(jnp.float32)
    d = d_ref[...] * (-LOG2E)
    for k in range(tiles):
        lanes = slice(k * LANES, (k + 1) * LANES)
        step_ref[k * tokens : (k + 1) * tokens, :] = step[:, lanes]
        grads[k * tokens : (k + 1) * tokens, :] = g[:, lanes]
        rate_ref[k * states : (k + 1) * states, :] = d[:, lanes]
    rate = [rate_ref[pl.ds(n, tiles, stride=states), :] for n in range(states)]

    def body(i, carry):
        total, held = carry
        t = tokens - 1 - i
        s = step_ref[pl.ds(t, tiles, stride=tokens), :]
        grad = grads[pl.ds(t, tiles, stride=tokens), :]
        held = tuple(
            jnp.exp2(s * rate[n]) * (out_coef[n, t] * grad + held[n]) for n in range(states)
        )
        return total + s, held

    zero = jnp.zeros((tiles, LANES), jnp.float32)
    total, held = lax.fori_loop(0, tokens, body, (zero, (zero,) * states), unroll=UNROLL)
    for n in range(states):
        state[pl.ds(n, tiles, stride=states), :] = held[n]
    half, rows = tiles // 2, tiles // 2 * states
    for part in range(2):
        message_ref[part, :rows, :] = state[part * rows : (part + 1) * rows, :]
        message_ref[part, rows : rows + tiles, :] = jnp.concatenate(
            [total[part * half : (part + 1) * half], zero[:half]], axis=0
        )


def first(out_coef, ids, gate, cot, x, w, b, d, g):
    tokens, inner = x.shape
    channels, states, width = w.shape[1], d.shape[0], cot.shape[1]
    steps, tiles = channels // TILE, TILE // LANES
    whole = lambda *shape: pl.BlockSpec(shape, lambda q: (0,) * len(shape))
    message = (2, tiles // 2 * states + tiles, LANES)
    return pl.pallas_call(
        first_kernel,
        grid=(steps,),
        in_specs=[
            pl.BlockSpec(memory_space=pltpu.SMEM),
            whole(*ids.shape),
            whole(*gate.shape),
            whole(*cot.shape),
            whole(tokens, inner),
            pl.BlockSpec((inner, TILE), lambda q: (0, q)),
            pl.BlockSpec((1, TILE), lambda q: (0, q)),
            pl.BlockSpec((states, TILE), lambda q: (0, q)),
            pl.BlockSpec((tokens, TILE), lambda q: (0, q)),
        ],
        out_specs=[
            whole(Y_SIZE, SLOTS, width // Y_SIZE),
            pl.BlockSpec((tiles * tokens, LANES), lambda q: (q, 0)),
            pl.BlockSpec(message, lambda q: (q, 0, 0)),
            pl.BlockSpec((tiles * states, LANES), lambda q: (q, 0)),
        ],
        out_shape=[
            jax.ShapeDtypeStruct((Y_SIZE, SLOTS, width // Y_SIZE), jnp.bfloat16),
            jax.ShapeDtypeStruct((steps * tiles * tokens, LANES), jnp.float32),
            jax.ShapeDtypeStruct((2 * steps,) + message[1:], jnp.float32),
            jax.ShapeDtypeStruct((steps * tiles * states, LANES), jnp.float32),
        ],
        scratch_shapes=[
            pltpu.VMEM((tiles * tokens, LANES), jnp.float32),
            pltpu.VMEM((tiles * states, LANES), jnp.float32),
        ],
        compiler_params=pltpu.CompilerParams(vmem_limit_bytes=VMEM_LIMIT),
        name="first",
    )(out_coef, ids, gate, cot, x, w, b, d, g)


def exchange_kernel(
    hidden_ref, routed_ref, message_ref, rate_ref, incoming_ref, down_ref,
    hidden, slices, rows, states, sums, arrived, partial, parts,
    hs, hr, ds, dr, zs, zr, fs, fr, ss, sr, ts, tr, ps, pr,
):
    i, j = lax.axis_index("dp"), lax.axis_index("seq")
    y, zx = i // 16, lax.rem(i, 16)
    zl, x = zx // 8, lax.rem(zx, 8)
    units = hidden_ref.shape[0]
    split = units // 2 // LANES * LANES + LANES
    chunks = ((0, split), (split, units - split))
    sibling = j + 1 - 2 * lax.rem(j, 2)

    def on_y(k):
        return {"dp": lax.rem(y + k, Y_SIZE) * 16 + zx, "seq": j}

    def on_seq(k):
        return {"dp": i, "seq": lax.rem(j + k, PEERS)}

    def on_plane(k):
        other = lax.rem(zl + k // 8, 2) * 8 + lax.rem(x + k % 8, 8)
        return other, {"dp": y * 16 + other, "seq": j}

    def copy(src, dst, send, recv, device):
        c = pltpu.make_async_remote_copy(
            src_ref=src, dst_ref=dst, send_sem=send, recv_sem=recv,
            device_id=device, device_id_type=MESH,
        )
        c.start()
        return c

    barrier = pltpu.get_barrier_semaphore()
    greeted = [on_y(k) for k in range(1, Y_SIZE)]
    greeted += [on_seq(k) for k in range(1, PEERS)]
    greeted += [on_plane(k)[1] for k in range(1, 16)]
    for device in greeted:
        pl.semaphore_signal(barrier, inc=1, device_id=device, device_id_type=MESH)
    pl.semaphore_wait(barrier, len(greeted))

    sliced = [
        copy(routed_ref.at[lax.rem(y + k, Y_SIZE)], slices.at[y], ds.at[k], dr.at[k], on_y(k))
        for k in range(1, Y_SIZE)
    ]
    told = [
        copy(message_ref.at[lax.rem(j + k, PEERS)], states.at[j], ss.at[k], sr.at[k], on_seq(k))
        for k in range(1, PEERS)
    ]
    gathered = {}

    def pass_on(hop, c):
        at, size = chunks[c]
        here = pl.ds(at, size)
        for way, last in ((0, 4), (1, 3)):
            if hop < last:
                slot = hop if way == 0 else (0 if hop == 0 else 4 + hop)
                land = hop + 1 if way == 0 else 5 + hop
                source = hidden_ref if hop == 0 else hidden.at[slot]
                gathered[hop, c, way] = copy(
                    source.at[here], hidden.at[land, here], hs.at[c, land], hr.at[c, land],
                    on_y(1 if way == 0 else Y_SIZE - 1),
                )

    def arrive(hop, c):
        for way in (0, 1):
            if (hop, c, way) in gathered:
                gathered[hop, c, way].wait_recv()

    for c in range(2):
        pass_on(0, c)
    slices[y] = routed_ref[y]
    states[j] = message_ref[j]

    for c in sliced:
        c.wait_recv()
    rows[:, j] = slices[...]
    spread = [
        copy(slices, rows.at[:, j], zs.at[k], zr.at[k], on_seq(2 * k)) for k in range(1, 4)
    ]
    spread.append(copy(slices, rows.at[:, j], zs.at[0], zr.at[0], {"dp": i, "seq": sibling}))
    for c in range(2):
        arrive(0, c)
        pass_on(1, c)

    for c in told:
        c.wait_recv()
    lines = rate_ref.shape[1]
    factor = rate_ref[j]
    block = lines // 4
    current = jnp.zeros((lines, LANES), jnp.float32)
    for b in reversed(range(PEERS)):
        sums[b] = current
        if b:
            total = jnp.concatenate(
                [
                    jnp.broadcast_to(states[b, lines + k : lines + k + 1, :], (block, LANES))
                    for k in range(4)
                ],
                axis=0,
            )
            current = states[b, :lines, :] + jnp.exp2(factor * total) * current
    returned = [
        copy(sums.at[lax.rem(j + k, PEERS)], arrived.at[j], ts.at[k], tr.at[k], on_seq(k))
        for k in range(1, PEERS)
    ]
    arrived[j] = sums[j]

    for c in range(2):
        arrive(1, c)
        pass_on(2, c)
    forwarded = []
    for k in range(1, 4):
        spread[k - 1].wait_recv()
        origin = lax.rem(j + PEERS - 2 * k, PEERS)
        forwarded.append(
            copy(rows.at[:, origin], rows.at[:, origin], fs.at[k], fr.at[k], {"dp": i, "seq": sibling})
        )
    for c in range(2):
        arrive(2, c)
        pass_on(3, c)
    spread[3].wait_recv()
    for c in forwarded:
        c.wait_recv()

    depth, width = rows.shape[1] * rows.shape[2], rows.shape[3]

    def term(slot, c):
        at, size = chunks[c]
        origin = lax.rem(y + Y_SIZE - slot, Y_SIZE) if slot <= 4 else lax.rem(y + slot - 4, Y_SIZE)
        left = rows[origin].reshape(depth, width)
        right = (hidden_ref if slot == 0 else hidden.at[slot])[pl.ds(at, size), :]
        return lax.dot_general(
            left, right, (((0,), (1,)), ((), ())), preferred_element_type=jnp.float32
        )

    early = []
    for c in range(2):
        total = term(0, c)
        for slot in (1, 2, 3, 5, 6, 7):
            total = total + term(slot, c)
        at, size = chunks[c]
        partial[:, :, at : at + size] = total.reshape(16, SLOTS, size)
    scattered = []
    for c in range(2):
        at, size = chunks[c]
        arrive(3, c)
        partial[:, :, at : at + size] += term(4, c).reshape(16, SLOTS, size)
        for k in range(1, 16):
            other, device = on_plane(k)
            scattered.append(
                copy(
                    partial.at[other, :, pl.ds(at, size)], parts.at[k, :, pl.ds(at, size)],
                    ps.at[c, k], pr.at[c, k], device,
                )
            )
    for c in returned:
        c.wait_recv()
    incoming_ref[...] = arrived[...]
    for c in range(2):
        at, size = chunks[c]
        total = partial[zx, :, at : at + size]
        for k in range(1, 16):
            scattered[c * 15 + k - 1].wait_recv()
            total = total + parts[k, :, at : at + size]
        down_ref[:, at : at + size] = total
    for c in sliced + told + list(gathered.values()) + spread + returned + forwarded + scattered:
        c.wait_send()


def exchange(hidden, routed, message, rate):
    units, depth = hidden.shape
    width = routed.shape[2]
    lines = rate.shape[1]
    vmem = pl.BlockSpec(memory_space=pltpu.VMEM)
    sem = pltpu.SemaphoreType.DMA
    return pl.pallas_call(
        exchange_kernel,
        in_specs=[vmem] * 4,
        out_specs=[vmem] * 2,
        out_shape=[
            jax.ShapeDtypeStruct((PEERS, lines, LANES), jnp.float32),
            jax.ShapeDtypeStruct((SLOTS, units), jnp.float32),
        ],
        scratch_shapes=[
            pltpu.VMEM((8, units, depth), jnp.bfloat16),
            pltpu.VMEM((Y_SIZE, SLOTS, width), jnp.bfloat16),
            pltpu.VMEM((Y_SIZE, PEERS, SLOTS, width), jnp.bfloat16),
            pltpu.VMEM(message.shape, jnp.float32),
            pltpu.VMEM((PEERS, lines, LANES), jnp.float32),
            pltpu.VMEM((PEERS, lines, LANES), jnp.float32),
            pltpu.VMEM((16, SLOTS, units), jnp.float32),
            pltpu.VMEM((16, SLOTS, units), jnp.float32),
            sem((2, 8)), sem((2, 8)),
            sem((8,)), sem((8,)),
            sem((4,)), sem((4,)),
            sem((4,)), sem((4,)),
            sem((8,)), sem((8,)),
            sem((8,)), sem((8,)),
            sem((2, 16)), sem((2, 16)),
        ],
        compiler_params=pltpu.CompilerParams(
            collective_id=0, has_side_effects=True, vmem_limit_bytes=VMEM_LIMIT
        ),
        name="exchange",
    )(hidden, routed, message, rate)


def last_kernel(
    out_coef, in_coef, step_ref, incoming_ref, rate_ref, g_ref, skip_ref, out_ref, grads, results
):
    tokens, tiles = g_ref.shape[0], TILE // LANES
    states = rate_ref.shape[0] // tiles
    g = g_ref[...].astype(jnp.float32)
    for k in range(tiles):
        grads[k * tokens : (k + 1) * tokens, :] = g[:, k * LANES : (k + 1) * LANES]
    rate = [rate_ref[pl.ds(n, tiles, stride=states), :] for n in range(states)]

    def body(i, held):
        t = tokens - 1 - i
        s = step_ref[pl.ds(t, tiles, stride=tokens), :]
        grad = grads[pl.ds(t, tiles, stride=tokens), :]
        after, sums = [], [None] * 4
        for n in range(states):
            adjoint = out_coef[n, t] * grad + held[n]
            product = in_coef[n, t] * adjoint
            sums[n % 4] = product if n < 4 else sums[n % 4] + product
            after.append(jnp.exp2(s * rate[n]) * adjoint)
        results[pl.ds(t, tiles, stride=tokens), :] = s * ((sums[0] + sums[1]) + (sums[2] + sums[3]))
        return tuple(after)

    held = tuple(incoming_ref[pl.ds(n, tiles, stride=states), :] for n in range(states))
    lax.fori_loop(0, tokens, body, held, unroll=UNROLL // 2)
    skip = skip_ref[...]
    for k in range(tiles):
        lanes = slice(k * LANES, (k + 1) * LANES)
        out_ref[:, lanes] = (
            results[k * tokens : (k + 1) * tokens, :] + skip[:, lanes] * g[:, lanes]
        ).astype(jnp.bfloat16)


def last(out_coef, in_coef, step, incoming, rate, g, skip):
    tokens, channels = g.shape
    steps, tiles = channels // TILE, TILE // LANES
    states = rate.shape[0] // (steps * tiles)
    return pl.pallas_call(
        last_kernel,
        grid=(steps,),
        in_specs=[
            pl.BlockSpec(memory_space=pltpu.SMEM),
            pl.BlockSpec(memory_space=pltpu.SMEM),
            pl.BlockSpec((tiles * tokens, LANES), lambda q: (q, 0)),
            pl.BlockSpec((tiles * states, LANES), lambda q: (q, 0)),
            pl.BlockSpec((tiles * states, LANES), lambda q: (q, 0)),
            pl.BlockSpec((tokens, TILE), lambda q: (0, q)),
            pl.BlockSpec((1, TILE), lambda q: (0, q)),
        ],
        out_specs=pl.BlockSpec((tokens, TILE), lambda q: (0, q)),
        out_shape=jax.ShapeDtypeStruct((tokens, channels), jnp.bfloat16),
        scratch_shapes=[
            pltpu.VMEM((tiles * tokens, LANES), jnp.float32),
            pltpu.VMEM((tiles * tokens, LANES), jnp.float32),
        ],
        compiler_params=pltpu.CompilerParams(vmem_limit_bytes=VMEM_LIMIT),
        name="last",
    )(out_coef, in_coef, step, incoming, rate, g, skip)


def on_device(
    cotangent, expert_ids, gate_probs, hidden_acts, step_input, step_proj, step_bias,
    decay_rate, input_coef, output_coef, grad_output, skip_weight,
):
    out_coef, in_coef, g = output_coef[0], input_coef[0], grad_output[0]
    routed, step, message, rate = first(
        out_coef, expert_ids[0], gate_probs[0], cotangent[0], step_input[0], step_proj,
        step_bias[None, :], decay_rate, g,
    )
    incoming, grad_down = exchange(hidden_acts, routed, message, rate.reshape(PEERS, -1, LANES))
    grad_x = last(
        out_coef, in_coef, step, incoming.reshape(-1, LANES), rate, g, skip_weight[None, :]
    )
    return (grad_down, grad_x[None])


def solution(mesh):
    return jax.shard_map(
        on_device,
        mesh=mesh,
        in_specs=(
            P("dp", "seq", None),
            P("dp", "seq", None),
            P("dp", "seq", None),
            P("seq", "dp"),
            P("dp", "seq", None),
            P(),
            P(),
            P(),
            P("dp", None, "seq"),
            P("dp", None, "seq"),
            P("dp", "seq", None),
            P(),
        ),
        out_specs=(P("dp", "seq"), P("dp", "seq", None)),
        check_vma=False,
    )
```

time: 691 us -> 108 us (0.16)
  the two profiles are of different devices: /device:TPU:256 before, /device:TPU:1 now
where the time goes in v1:
time: 108 us; the launch traced here: 107 us
  Pallas kernels  97.4 us (90%)
  local copies, waits for them, and re-layouts  9.26 us (9%)
    pallas_call x1, Pallas kernels, exchange(): pl.pallas_call(exchange_kernel, in_specs=[vmem] * 4, out_specs=[vmem] * 2...  70.5 us
    pallas_call x1, Pallas kernels, last(): pl.pallas_call(last_kernel, grid=(steps,), in_specs=[pl.BlockSpec(memory_...  15.1 us
    pallas_call x1, Pallas kernels, first(): pl.pallas_call(first_kernel, grid=(steps,), in_specs=[pl.BlockSpec(memory...  11.9 us
    unnamed x25, local copies, waits for them, and re-layouts  9.26 us

profile of v1, /device:TPU:1, one launch (start us, length us, event | category | flops | bytes accessed | tf_op | source)
XLA Modules:
  0.0 107.4 jit_solution(18249839561358261433)
XLA Ops:
  0.6 0.8 copy.14
  1.4 0.8 copy.15
  2.2 0.0 copy-start
  2.2 1.2 %copy-done = bf16[1,128,4096]{2,1,0:T(8,128)(2,1)S(1)} copy-done((bf16[1,128,4096]{2,1,0:T(8,128)(2,1)S(1)}, bf16[1,128,4096]{2,1,0:T(8,128)(2,1)}, u32[]{:S(2)}) %copy-start) | copy-done | bytes 1048600
  3.4 0.0 copy-start.2
  3.4 1.6 %copy-done.2 = bf16[256,4096]{1,0:T(8,128)(2,1)S(1)} copy-done((bf16[256,4096]{1,0:T(8,128)(2,1)S(1)}, bf16[256,4096]{1,0:T(8,128)(2,1)}, u32[]{:S(2)}) %copy-start.2) | copy-done | bytes 2097176
  5.0 0.0 copy-start.3
  5.0 1.0 copy-done.3
  6.1 0.0 copy-start.4
  6.1 0.9 copy-done.4
  7.0 0.0 copy-start.6
  7.0 0.8 copy-done.6
  7.8 0.0 copy-start.7
  7.9 0.7 copy-done.7
  8.5 0.0 copy-start.8
  8.5 0.7 copy-done.8
  9.3 0.0 copy-start.5
  9.3 0.0 copy-start.1
  9.3 0.0 copy-start.9
  9.3 0.0 copy-start.10
  9.3 11.9 %first.1 = (bf16[8,16,256]{2,1,0:T(8,128)(2,1)S(1)}, f32[4096,128]{1,0:T(8,128)S(1)}, f32[8,72,128]{2,1,0:T(8,128)S(1)}, f32[512,128]{1,0:T(8,128)S(1)}) custom-call(f32[16,128]{1,0:T(8,128)S(1)} %bitcast.20, s32[128,2]{1,0:T(8,128)S(1)} %bitcast.16, f32[128,2]{1,0:T(8,128)S(1)} %bitcast.17, bf16[128,2048]{1,0:T(8,128)(2,1)S(1)} %bitcast.15, ...), custom_call_target="tpu_custom_call" | custom-call | tf_op jit(solution)/shard_map/first/pallas_call | solution.py:98
  21.1 0.0 copy-done.5
  21.2 70.5 %exchange.1 = (f32[8,64,128]{2,1,0:T(8,128)S(1)}, f32[16,896]{1,0:T(8,128)S(1)}) custom-call(bf16[896,128]{1,0:T(8,128)(2,1)S(1)} %copy-done.5, bf16[8,16,256]{2,1,0:T(8,128)(2,1)S(1)} %get-tuple-element.8.routed_ref, f32[8,72,128]{2,1,0:T(8,128)S(1)} %get-tuple-element.9.message_ref, f32[8,64,128]{2,1,0:T(8,128)S(1)} %bitcast.14), custom_call_target="tpu_custom_call" | custom-call | tf_op jit(solution)/shard_map/exchange/pallas_call | solution.py:307
  91.6 0.0 copy-done.1
  91.6 0.0 copy-done.9
  91.7 0.0 copy-done.10
  91.7 15.1 %last.1 = bf16[128,4096]{1,0:T(8,128)(2,1)} custom-call(f32[16,128]{1,0:T(8,128)S(1)} %bitcast.21, f32[16,128]{1,0:T(8,128)S(1)} %bitcast.24, f32[4096,128]{1,0:T(8,128)S(1)} %get-tuple-element.12.step_ref, f32[512,128]{1,0:T(8,128)S(1)} %bitcast.18, f32[512,128]{1,0:T(8,128)S(1)} %get-tuple-element.10.rate_ref, bf16[128,4096]{1,0:T(8,128)(2,1)S(1)} %bitcast.13, ...), custom_call_target="tpu_custom_call" | custom-call | tf_op jit(solution)/shard_map/last/pallas_call | solution.py:376
  106.8 0.6 copy.17
Async XLA Ops:
  2.2 1.2 %copy-start = (bf16[1,128,4096]{2,1,0:T(8,128)(2,1)S(1)}, bf16[1,128,4096]{2,1,0:T(8,128)(2,1)}, u32[]{:S(2)}) copy-start(bf16[1,128,4096]{2,1,0:T(8,128)(2,1)} %param.22) | copy-start | bytes 3145732
  3.4 1.6 %copy-start.2 = (bf16[256,4096]{1,0:T(8,128)(2,1)S(1)}, bf16[256,4096]{1,0:T(8,128)(2,1)}, u32[]{:S(2)}) copy-start(bf16[256,4096]{1,0:T(8,128)(2,1)} %w_ref.1) | copy-start | bytes 6291460
  5.0 1.0 copy-start.3
  6.1 0.9 copy-start.4
  7.0 0.8 copy-start.6
  7.8 0.7 copy-start.7
  8.5 0.7 copy-start.8
  9.3 11.9 %copy-start.5 = (bf16[896,128]{1,0:T(8,128)(2,1)S(1)}, bf16[896,128]{1,0:T(8,128)(2,1)}, u32[]{:S(2)}) copy-start(bf16[896,128]{1,0:T(8,128)(2,1)} %hidden_ref.1) | copy-start | bytes 688132
  9.3 82.4 %copy-start.1 = (bf16[1,128,4096]{2,1,0:T(8,128)(2,1)S(1)}, bf16[1,128,4096]{2,1,0:T(8,128)(2,1)}, u32[]{:S(2)}) copy-start(bf16[1,128,4096]{2,1,0:T(8,128)(2,1)} %param.22) | copy-start | bytes 3145732
  9.3 82.4 %copy-start.9 = (f32[4096]{0:T(1024)S(1)}, f32[4096]{0:T(1024)}, u32[]{:S(2)}) copy-start(f32[4096]{0:T(1024)} %param.23) | copy-start | bytes 49156
  9.3 82.4 %copy-start.10 = (f32[1,16,128]{2,1,0:T(8,128)S(1)}, f32[1,16,128]{2,1,0:T(8,128)}, u32[]{:S(2)}) copy-start(f32[1,16,128]{2,1,0:T(8,128)} %param.20) | copy-start | bytes 24580

commit v2 on v0

v2 whole, which is shorter than its diff:
```python
import functools
import math

import jax
import jax.numpy as jnp
from jax import lax
from jax.experimental import pallas as pl
from jax.experimental.pallas import tpu as pltpu
from jax.sharding import PartitionSpec as P

MESH = pl.DeviceIdType.MESH
LANES = 128
TILE = 8 * LANES
LOG2E = math.log2(math.e)
UNROLL = 4
X_SIZE = 8
Y_SIZE = 8
PEERS = 8
SLOTS = 16
VMEM_LIMIT = 56 << 20


def softplus(v):
    return jnp.maximum(v, 0.0) + jnp.log1p(jnp.exp(-jnp.abs(v)))


def route(ids_ref, gate_ref, cot_ref, routed_ref):
    tokens = cot_ref.shape[0]
    named = (ids_ref[...] == 0).astype(jnp.float32)
    chosen = jnp.sum(named, axis=0, keepdims=True)
    gate = jnp.sum(named * gate_ref[...], axis=0, keepdims=True)
    row = lax.broadcasted_iota(jnp.int32, (tokens, tokens), 0)
    col = lax.broadcasted_iota(jnp.int32, (tokens, tokens), 1)
    earlier = jnp.where(row < col, 1.0, 0.0).astype(jnp.bfloat16)
    spread = jnp.broadcast_to(chosen, (SLOTS, tokens))
    rank = jnp.dot(spread.astype(jnp.bfloat16), earlier, preferred_element_type=jnp.float32)
    slot = lax.broadcasted_iota(jnp.int32, (SLOTS, tokens), 0).astype(jnp.float32)
    pick = jnp.where(rank == slot, spread, 0.0)
    weight = jnp.sum(pick * gate, axis=1, keepdims=True)
    width = routed_ref.shape[2]
    for y in range(routed_ref.shape[0]):
        picked = jnp.dot(
            pick.astype(jnp.bfloat16),
            cot_ref[:, y * width : (y + 1) * width],
            preferred_element_type=jnp.float32,
        )
        routed_ref[y] = (weight * picked).astype(jnp.bfloat16)


def fused_kernel(
    out_coef, in_coef, ids_hbm, gate_hbm, cot_hbm, hid_hbm, x_hbm, w_hbm, b_hbm, d_hbm, g_hbm, skip_hbm,
    down_hbm, gx_hbm,
    ids_ref, gate_ref, cot_ref, hid_ref, x_ref, w_ref, b_ref, d_ref, g_ref, skip_ref, down_ref, gx_ref,
    routed_ref, steps, grads, rates, message, told, sums, arrived, results,
    hidden, slices, rows, partial, rounded, parts,
    local, hs, hr, ds, dr, zs, zr, fs, fr, ss, sr, ts, tr, ps, pr,
):
    i, j = lax.axis_index("dp"), lax.axis_index("seq")
    y, zx = i // 16, lax.rem(i, 16)
    zl, x = zx // 8, lax.rem(zx, 8)
    units = hid_ref.shape[0]
    split = units // 2 // LANES * LANES + LANES
    chunks = ((0, split), (split, units - split))
    sibling = j + 1 - 2 * lax.rem(j, 2)
    tokens, states, tiles = x_ref.shape[0], d_ref.shape[0], TILE // LANES
    quarters = w_ref.shape[1] // TILE
    pairs = quarters // 2
    sent = told.shape[2]
    lines = 2 * states

    def fetch(k, src, dst):
        c = pltpu.make_async_copy(src, dst, local.at[k])
        c.start()
        return c

    def columns(q):
        return pl.ds(q * TILE, TILE)

    small = [
        fetch(0, ids_hbm, ids_ref), fetch(1, gate_hbm, gate_ref), fetch(2, cot_hbm, cot_ref),
        fetch(3, x_hbm, x_ref), fetch(4, b_hbm, b_ref), fetch(5, d_hbm, d_ref), fetch(6, skip_hbm, skip_ref),
    ]
    weights, outputs = [], []
    for q in range(quarters):
        weights.append(fetch(8 + q, w_hbm.at[:, columns(q)], w_ref.at[:, columns(q)]))
        outputs.append(fetch(12 + q, g_hbm.at[:, columns(q)], g_ref.at[:, columns(q)]))
    held_units = fetch(7, hid_hbm, hid_ref)

    def on_y(k):
        return {"dp": lax.rem(y + k, Y_SIZE) * 16 + zx, "seq": j}

    def on_seq(k):
        return {"dp": i, "seq": lax.rem(j + k, PEERS)}

    def on_plane(k):
        other = lax.rem(zl + k // 8, 2) * 8 + lax.rem(x + k % 8, 8)
        return other, {"dp": y * 16 + other, "seq": j}

    barrier = pltpu.get_barrier_semaphore()
    greeted = [on_y(k) for k in range(1, Y_SIZE)]
    greeted += [on_seq(k) for k in range(1, PEERS)]
    greeted += [on_plane(k)[1] for k in range(1, 16)]
    for device in greeted:
        pl.semaphore_signal(barrier, inc=1, device_id=device, device_id_type=MESH)

    started = []

    def copy(src, dst, send, recv, device):
        c = pltpu.make_async_remote_copy(
            src_ref=src, dst_ref=dst, send_sem=send, recv_sem=recv,
            device_id=device, device_id_type=MESH,
        )
        c.start()
        started.append(c)
        return c

    gathered = {}

    def pass_on(hop):
        for c in range(2):
            at, size = chunks[c]
            here = pl.ds(at, size)
            for way, final in ((0, 4), (1, 3)):
                if hop < final:
                    if hop:
                        gathered[hop - 1, c, way].wait_recv()
                    slot = hop if way == 0 else 4 + hop
                    land = hop + 1 if way == 0 else 5 + hop
                    source = hid_ref if hop == 0 else hidden.at[slot]
                    gathered[hop, c, way] = copy(
                        source.at[here], hidden.at[land, here], hs.at[c, land], hr.at[c, land],
                        on_y(1 if way == 0 else Y_SIZE - 1),
                    )

    def prepare(q):
        weights[q].wait()
        outputs[q].wait()
        own = slice(q * TILE, (q + 1) * TILE)
        step = softplus(
            jnp.dot(x_ref[...], w_ref[:, own], preferred_element_type=jnp.float32) + b_ref[:, own]
        )
        g = g_ref[:, own].astype(jnp.float32)
        d = d_ref[:, own] * (-LOG2E)
        for k in range(tiles):
            lanes = slice(k * LANES, (k + 1) * LANES)
            steps[q, k * tokens : (k + 1) * tokens, :] = step[:, lanes]
            grads[q, k * tokens : (k + 1) * tokens, :] = g[:, lanes]
            rates[q, k * states : (k + 1) * states, :] = d[:, lanes]

    def rate_of(q):
        return [rates[q, pl.ds(n, tiles, stride=states), :] for n in range(states)]

    def at_token(ref, q, t):
        return ref[q, pl.ds(t, tiles, stride=tokens), :]

    zero = jnp.zeros((tiles, LANES), jnp.float32)

    def scan_states(q, half, carry):
        rate = rate_of(q)
        count = tokens // 2

        def body(k, carry):
            total, held = carry
            t = tokens - 1 - half * count - k
            s, grad = at_token(steps, q, t), at_token(grads, q, t)
            held = tuple(
                jnp.exp2(s * rate[n]) * (out_coef[n, t] * grad + held[n]) for n in range(states)
            )
            return total + s, held

        return lax.fori_loop(0, count, body, carry, unroll=UNROLL)

    def finish_states(q, carry):
        total, held = carry
        for n in range(states):
            message[q // 2, pl.ds(q % 2 * states + n, tiles, stride=sent), :] = held[n]
        message[q // 2, pl.ds(lines + q % 2, tiles, stride=sent), :] = total

    def scan_states_whole(q):
        finish_states(q, scan_states(q, 1, scan_states(q, 0, (zero, (zero,) * states))))

    def tell(a):
        return [
            copy(
                message.at[a, pl.ds(pl.multiple_of(lax.rem(j + k, PEERS) * sent, 8), sent), :],
                told.at[a, j], ss.at[a, k], sr.at[a, k], on_seq(k),
            )
            for k in range(1, PEERS)
        ]

    def combine(a, incoming):
        told[a, j] = message[a, pl.ds(pl.multiple_of(j * sent, 8), sent), :]
        mine = pl.ds(pl.multiple_of(j * states, 8), states)
        factor = jnp.concatenate([rates[2 * a, mine, :], rates[2 * a + 1, mine, :]], axis=0)
        for c in incoming:
            c.wait_recv()
        current = jnp.zeros((lines, LANES), jnp.float32)
        for b in reversed(range(PEERS)):
            sums[a, b] = current
            if b:
                total = jnp.concatenate(
                    [
                        jnp.broadcast_to(told[a, b, lines + k : lines + k + 1, :], (states, LANES))
                        for k in range(2)
                    ],
                    axis=0,
                )
                current = told[a, b, :lines, :] + jnp.exp2(factor * total) * current
        slot = pl.ds(pl.multiple_of(j * lines, 8), lines)
        back = [
            copy(
                sums.at[a, lax.rem(j + k, PEERS)], arrived.at[a, slot, :], ts.at[a, k], tr.at[a, k], on_seq(k)
            )
            for k in range(1, PEERS)
        ]
        arrived[a, slot, :] = sums[a, j]
        return back

    def scan_outputs(q):
        rate = rate_of(q)

        def body(k, held):
            t = tokens - 1 - k
            s, grad = at_token(steps, q, t), at_token(grads, q, t)
            after, total = [], [None] * 4
            for n in range(states):
                adjoint = out_coef[n, t] * grad + held[n]
                product = in_coef[n, t] * adjoint
                total[n % 4] = product if n < 4 else total[n % 4] + product
                after.append(jnp.exp2(s * rate[n]) * adjoint)
            results[pl.ds(t, tiles, stride=tokens), :] = s * ((total[0] + total[1]) + (total[2] + total[3]))
            return tuple(after)

        held = tuple(
            arrived[q // 2, pl.ds(q % 2 * states + n, tiles, stride=lines), :] for n in range(states)
        )
        lax.fori_loop(0, tokens, body, held, unroll=UNROLL)
        for k in range(tiles):
            lanes = slice(q * TILE + k * LANES, q * TILE + (k + 1) * LANES)
            gx_ref[:, lanes] = (
                results[k * tokens : (k + 1) * tokens, :]
                + skip_ref[:, lanes] * g_ref[:, lanes].astype(jnp.float32)
            ).astype(jnp.bfloat16)
        return fetch(q, gx_ref.at[:, columns(q)], gx_hbm.at[:, columns(q)])

    depth, width = rows.shape[1] * rows.shape[2], rows.shape[3]

    def accumulate(slots):
        for c in range(2):
            at, size = chunks[c]
            total = None
            for slot in slots:
                origin = lax.rem(y + Y_SIZE - slot, Y_SIZE) if slot <= 4 else lax.rem(y + slot - 4, Y_SIZE)
                left = rows[origin].reshape(depth, width)
                right = (hid_ref if slot == 0 else hidden.at[slot])[pl.ds(at, size), :]
                term = lax.dot_general(
                    left, right, (((0,), (1,)), ((), ())), preferred_element_type=jnp.float32
                )
                total = term if total is None else total + term
            total = total.reshape(16, SLOTS, size)
            if 0 in slots:
                partial[:, :, at : at + size] = total
            else:
                partial[:, :, at : at + size] += total

    message[...] = jnp.zeros_like(message)
    for c in small:
        c.wait()
    route(ids_ref, gate_ref, cot_ref, routed_ref)
    prepare(0)
    scan_states_whole(0)
    held_units.wait()
    pl.semaphore_wait(barrier, len(greeted))

    sliced = [
        copy(routed_ref.at[lax.rem(y + k, Y_SIZE)], slices.at[y], ds.at[k], dr.at[k], on_y(k))
        for k in range(1, Y_SIZE)
    ]
    pass_on(0)
    slices[y] = routed_ref[y]
    prepare(1)
    scan_states_whole(1)
    first_told = tell(0)
    for c in sliced:
        c.wait_recv()
    rows[:, j] = slices[...]
    spread = [
        copy(slices, rows.at[:, j], zs.at[k], zr.at[k], on_seq(2 * k)) for k in range(1, 4)
    ]
    spread.append(copy(slices, rows.at[:, j], zs.at[0], zr.at[0], {"dp": i, "seq": sibling}))
    prepare(2)
    carry = scan_states(2, 0, (zero, (zero,) * states))
    pass_on(1)
    finish_states(2, scan_states(2, 1, carry))
    prepare(3)
    scan_states_whole(3)
    second_told = tell(1)
    first_back = combine(0, first_told)
    pass_on(2)
    forwarded = []
    for k in range(1, 4):
        spread[k - 1].wait_recv()
        origin = lax.rem(j + PEERS - 2 * k, PEERS)
        forwarded.append(
            copy(rows.at[:, origin], rows.at[:, origin], fs.at[k], fr.at[k], {"dp": i, "seq": sibling})
        )
    spread[3].wait_recv()
    for c in forwarded:
        c.wait_recv()
    accumulate((0, 1, 5))
    second_back = combine(1, second_told)
    pass_on(3)
    for c in first_back:
        c.wait_recv()
    done = [scan_outputs(0)]
    for c in range(2):
        gathered[2, c, 1].wait_recv()
    accumulate((2, 3, 6, 7))
    for c in range(2):
        gathered[3, c, 0].wait_recv()
    accumulate((4,))
    rounded[...] = partial[...].astype(jnp.bfloat16)
    scattered = []
    for c in range(2):
        at, size = chunks[c]
        for k in range(1, 16):
            other, device = on_plane(k)
            scattered.append(
                copy(
                    rounded.at[other, :, pl.ds(at, size)], parts.at[k, :, pl.ds(at, size)],
                    ps.at[c, k], pr.at[c, k], device,
                )
            )
    done.append(scan_outputs(1))
    for c in second_back:
        c.wait_recv()
    done.append(scan_outputs(2))
    done.append(scan_outputs(3))
    for c in range(2):
        at, size = chunks[c]
        total = partial[zx, :, at : at + size]
        for k in range(1, 16):
            scattered[c * 15 + k - 1].wait_recv()
            total = total + parts[k, :, at : at + size].astype(jnp.float32)
        down_ref[:, at : at + size] = total
    done.append(fetch(4, down_ref, down_hbm))
    for c in started:
        c.wait_send()
    for c in done:
        c.wait()


def fused(out_coef, in_coef, ids, gate, cot, hid, x, w, b, d, g, skip):
    units, depth = hid.shape
    tokens, width = cot.shape
    width = width // Y_SIZE
    channels, states = w.shape[1], d.shape[0]
    quarters, tiles = channels // TILE, TILE // LANES
    sent, lines = 2 * states + 8, 2 * states
    hbm = pl.BlockSpec(memory_space=pl.ANY)
    smem = pl.BlockSpec(memory_space=pltpu.SMEM)
    sem, f32, bf16 = pltpu.SemaphoreType.DMA, jnp.float32, jnp.bfloat16
    arrays = (ids, gate, cot, hid, x, w, b, d, g, skip)
    return pl.pallas_call(
        fused_kernel,
        in_specs=[smem] * 2 + [hbm] * len(arrays),
        out_specs=[hbm] * 2,
        out_shape=[
            jax.ShapeDtypeStruct((SLOTS, units), f32),
            jax.ShapeDtypeStruct((tokens, channels), bf16),
        ],
        scratch_shapes=[pltpu.VMEM(a.shape, a.dtype) for a in arrays] + [
            pltpu.VMEM((SLOTS, units), f32),
            pltpu.VMEM((tokens, channels), bf16),
            pltpu.VMEM((Y_SIZE, SLOTS, width), bf16),
            pltpu.VMEM((quarters, tiles * tokens, LANES), f32),
            pltpu.VMEM((quarters, tiles * tokens, LANES), f32),
            pltpu.VMEM((quarters, tiles * states, LANES), f32),
            pltpu.VMEM((2, PEERS * sent, LANES), f32),
            pltpu.VMEM((2, PEERS, sent, LANES), f32),
            pltpu.VMEM((2, PEERS, lines, LANES), f32),
            pltpu.VMEM((2, PEERS * lines, LANES), f32),
            pltpu.VMEM((tiles * tokens, LANES), f32),
            pltpu.VMEM((8, units, depth), bf16),
            pltpu.VMEM((Y_SIZE, SLOTS, width), bf16),
            pltpu.VMEM((Y_SIZE, PEERS, SLOTS, width), bf16),
            pltpu.VMEM((16, SLOTS, units), f32),
            pltpu.VMEM((16, SLOTS, units), bf16),
            pltpu.VMEM((16, SLOTS, units), bf16),
            sem((16,)),
            sem((2, 8)), sem((2, 8)),
            sem((8,)), sem((8,)),
            sem((4,)), sem((4,)),
            sem((4,)), sem((4,)),
            sem((2, 8)), sem((2, 8)),
            sem((2, 8)), sem((2, 8)),
            sem((2, 16)), sem((2, 16)),
        ],
        compiler_params=pltpu.CompilerParams(
            collective_id=0, has_side_effects=True, vmem_limit_bytes=VMEM_LIMIT
        ),
        name="fused",
    )(out_coef, in_coef, *arrays)


def on_device(
    cotangent, expert_ids, gate_probs, hidden_acts, step_input, step_proj, step_bias,
    decay_rate, input_coef, output_coef, grad_output, skip_weight,
):
    grad_down, grad_x = fused(
        output_coef[0], input_coef[0], expert_ids[0].T, gate_probs[0].T, cotangent[0], hidden_acts,
        step_input[0], step_proj, step_bias[None, :], decay_rate, grad_output[0], skip_weight[None, :],
    )
    return (grad_down, grad_x[None])


def solution(mesh):
    return jax.shard_map(
        on_device,
        mesh=mesh,
        in_specs=(
            P("dp", "seq", None),
            P("dp", "seq", None),
            P("dp", "seq", None),
            P("seq", "dp"),
            P("dp", "seq", None),
            P(),
            P(),
            P(),
            P("dp", None, "seq"),
            P("dp", None, "seq"),
            P("dp", "seq", None),
            P(),
        ),
        out_specs=(P("dp", "seq"), P("dp", "seq", None)),
        check_vma=False,
    )
```

time: 691 us -> 71.4 us (0.10)
  the two profiles are of different devices: /device:TPU:256 before, /device:TPU:1 now
where the time goes in v2:
time: 71.4 us; the launch traced here: 71.1 us
  Pallas kernels  66.7 us (93%)
  local copies, waits for them, and re-layouts  3.73 us (5%)
    pallas_call x1, Pallas kernels, fused(): pl.pallas_call(fused_kernel, in_specs=[smem] * 2 + [hbm] * len(arrays), o...  66.7 us
    unnamed x2, local copies, waits for them, and re-layouts  3.73 us

profile of v2, /device:TPU:1, one launch (start us, length us, event | category | flops | bytes accessed | tf_op | source)
XLA Modules:
  0.0 71.1 jit_solution(15020938795330125225)
XLA Ops:
  0.6 66.7 %fused.1 = (f32[16,896]{1,0:T(8,128)}, bf16[128,4096]{1,0:T(8,128)(2,1)}) custom-call(f32[16,128]{1,0:T(8,128)} %bitcast.20, f32[16,128]{1,0:T(8,128)} %bitcast.21, s32[2,128]{1,0:T(2,128)} %bitcast.22, f32[2,128]{1,0:T(2,128)} %bitcast.23, bf16[128,2048]{1,0:T(8,128)(2,1)} %bitcast.16, bf16[896,128]{1,0:T(8,128)(2,1)} %hid_hbm.1, ...), custom_call_target="tpu_custom_call" | custom-call | tf_op jit(solution)/shard_map/fused/pallas_call | solution.py:364
  67.4 1.4 %copy.16 = f32[16,896]{1,0:T(8,128)} copy(f32[16,896]{1,0:T(8,128)} %get-tuple-element.8) | data formatting | bytes 114688
  68.8 2.3 %copy.17 = bf16[1,128,4096]{2,1,0:T(8,128)(2,1)} copy(bf16[1,128,4096]{2,1,0:T(8,128)(2,1)} %bitcast.14) | data formatting | bytes 2097152

commit v3 on v2

--- a/solution.py
+++ b/solution.py
@@ -18,6 +18,7 @@
 PEERS = 8
 SLOTS = 16
 VMEM_LIMIT = 56 << 20
+PAD = 8
 
 
 def softplus(v):
@@ -73,6 +74,9 @@
         c.start()
         return c
 
+    def span(k):
+        return slice(k * (tokens + PAD), k * (tokens + PAD) + tokens)
+
     def columns(q):
         return pl.ds(q * TILE, TILE)
 
@@ -143,15 +147,15 @@
         d = d_ref[:, own] * (-LOG2E)
         for k in range(tiles):
             lanes = slice(k * LANES, (k + 1) * LANES)
-            steps[q, k * tokens : (k + 1) * tokens, :] = step[:, lanes]
-            grads[q, k * tokens : (k + 1) * tokens, :] = g[:, lanes]
+            steps[q, span(k), :] = step[:, lanes]
+            grads[q, span(k), :] = g[:, lanes]
             rates[q, k * states : (k + 1) * states, :] = d[:, lanes]
 
     def rate_of(q):
         return [rates[q, pl.ds(n, tiles, stride=states), :] for n in range(states)]
 
     def at_token(ref, q, t):
-        return ref[q, pl.ds(t, tiles, stride=tokens), :]
+        return ref[q, pl.ds(t, tiles, stride=tokens + PAD), :]
 
     zero = jnp.zeros((tiles, LANES), jnp.float32)
 
@@ -228,7 +232,7 @@
                 product = in_coef[n, t] * adjoint
                 total[n % 4] = product if n < 4 else total[n % 4] + product
                 after.append(jnp.exp2(s * rate[n]) * adjoint)
-            results[pl.ds(t, tiles, stride=tokens), :] = s * ((total[0] + total[1]) + (total[2] + total[3]))
+            results[pl.ds(t, tiles, stride=tokens + PAD), :] = s * ((total[0] + total[1]) + (total[2] + total[3]))
             return tuple(after)
 
         held = tuple(
@@ -238,15 +242,15 @@
         for k in range(tiles):
             lanes = slice(q * TILE + k * LANES, q * TILE + (k + 1) * LANES)
             gx_ref[:, lanes] = (
-                results[k * tokens : (k + 1) * tokens, :]
+                results[span(k), :]
                 + skip_ref[:, lanes] * g_ref[:, lanes].astype(jnp.float32)
             ).astype(jnp.bfloat16)
         return fetch(q, gx_ref.at[:, columns(q)], gx_hbm.at[:, columns(q)])
 
     depth, width = rows.shape[1] * rows.shape[2], rows.shape[3]
 
-    def accumulate(slots):
-        for c in range(2):
+    def accumulate(slots, which=(0, 1)):
+        for c in which:
             at, size = chunks[c]
             total = None
             for slot in slots:
@@ -316,13 +320,12 @@
     for c in range(2):
         gathered[2, c, 1].wait_recv()
     accumulate((2, 3, 6, 7))
-    for c in range(2):
-        gathered[3, c, 0].wait_recv()
-    accumulate((4,))
-    rounded[...] = partial[...].astype(jnp.bfloat16)
     scattered = []
     for c in range(2):
         at, size = chunks[c]
+        gathered[3, c, 0].wait_recv()
+        accumulate((4,), (c,))
+        rounded[:, :, at : at + size] = partial[:, :, at : at + size].astype(jnp.bfloat16)
         for k in range(1, 16):
             other, device = on_plane(k)
             scattered.append(
@@ -373,14 +376,14 @@
             pltpu.VMEM((SLOTS, units), f32),
             pltpu.VMEM((tokens, channels), bf16),
             pltpu.VMEM((Y_SIZE, SLOTS, width), bf16),
-            pltpu.VMEM((quarters, tiles * tokens, LANES), f32),
-            pltpu.VMEM((quarters, tiles * tokens, LANES), f32),
+            pltpu.VMEM((quarters, tiles * (tokens + PAD), LANES), f32),
+            pltpu.VMEM((quarters, tiles * (tokens + PAD), LANES), f32),
             pltpu.VMEM((quarters, tiles * states, LANES), f32),
             pltpu.VMEM((2, PEERS * sent, LANES), f32),
             pltpu.VMEM((2, PEERS, sent, LANES), f32),
             pltpu.VMEM((2, PEERS, lines, LANES), f32),
             pltpu.VMEM((2, PEERS * lines, LANES), f32),
-            pltpu.VMEM((tiles * tokens, LANES), f32),
+            pltpu.VMEM((tiles * (tokens + PAD), LANES), f32),
             pltpu.VMEM((8, units, depth), bf16),
             pltpu.VMEM((Y_SIZE, SLOTS, width), bf16),
             pltpu.VMEM((Y_SIZE, PEERS, SLOTS, width), bf16),

time: 71.4 us -> 70.2 us (0.983)
  Pallas kernels: 66.7 us -> 65.5 us
    pallas_call x1, Pallas kernels: 66.7 us -> 65.5 us  [fused(): pl.pallas_call(fused_kernel, in_specs=[smem] * 2 + [hbm] * len(arrays), o...]
where the time goes in v3:
time: 70.2 us; the launch traced here: 69.9 us
  Pallas kernels  65.5 us (93%)
  local copies, waits for them, and re-layouts  3.73 us (5%)
    pallas_call x1, Pallas kernels, fused(): pl.pallas_call(fused_kernel, in_specs=[smem] * 2 + [hbm] * len(arrays), o...  65.5 us
    unnamed x2, local copies, waits for them, and re-layouts  3.73 us

profile of v3, /device:TPU:1, one launch (start us, length us, event | category | flops | bytes accessed | tf_op | source)
XLA Modules:
  0.0 69.9 jit_solution(1278084352223549476)
XLA Ops:
  0.6 65.5 %fused.1 = (f32[16,896]{1,0:T(8,128)}, bf16[128,4096]{1,0:T(8,128)(2,1)}) custom-call(f32[16,128]{1,0:T(8,128)} %bitcast.20, f32[16,128]{1,0:T(8,128)} %bitcast.21, s32[2,128]{1,0:T(2,128)} %bitcast.22, f32[2,128]{1,0:T(2,128)} %bitcast.23, bf16[128,2048]{1,0:T(8,128)(2,1)} %bitcast.16, bf16[896,128]{1,0:T(8,128)(2,1)} %hid_hbm.1, ...), custom_call_target="tpu_custom_call" | custom-call | tf_op jit(solution)/shard_map/fused/pallas_call | solution.py:367
  66.2 1.4 %copy.16 = f32[16,896]{1,0:T(8,128)} copy(f32[16,896]{1,0:T(8,128)} %get-tuple-element.8) | data formatting | bytes 114688
  67.6 2.3 %copy.17 = bf16[1,128,4096]{2,1,0:T(8,128)(2,1)} copy(bf16[1,128,4096]{2,1,0:T(8,128)(2,1)} %bitcast.14) | data formatting | bytes 2097152
